TPU v7x, 32 devices: a whole 2x2x4 slice. The times are simulated.
32 devices in a mesh: req: 16 (over z, y, core), tp: 2 (over x).
Axes of the slice: x: 2, y: 2, z: 4, core: 2. Of those that a mesh axis runs over, the one named last changes fastest.
Arguments:
- queries: bfloat16 [1024, 2048], P('req', 'tp'), may hold values from -18 to 18
- fresh_key_value: bfloat16 [1024, 1024], P('req', 'tp'), may hold values from -6 to 6
- key_value_cache: bfloat16 [64, 128, 1024], P('req', None, 'tp'), may hold values from -12.2 to 12.2
- request_page_index: int32 [144, 4], P('req'), may hold values from 0 to 3
- cache_length_rows: int32 [144], P('req'), may hold values from 2 to 512, as said below
- residual: bfloat16 [1024, 2048], P('req'), may hold values from -12.8 to 12.8
- w_out: bfloat16 [2048, 2048], P('tp'), may hold values from -0.125 to 0.125
- gain_in: float32 [2048], replicated, may hold values from 0.5 to 1.5
- route_ids: int32 [1024, 8], P('req'), may hold values from 0 to 15, all different within a row; in each aligned block of 32 rows (0 to 31, 32 to 63, ...) at most 32 rows name the same one
- route_weights: float32 [1024, 8], P('req'), may hold values from 0.1 to 1
- expert_home: int32 [16], replicated, may hold values from 0 to 15, each once
- w_gate: bfloat16 [16, 2048, 768], P('req', None, 'tp'), may hold values from -0.125 to 0.125
- w_up: bfloat16 [16, 2048, 768], P('req', None, 'tp'), may hold values from -0.125 to 0.125
- w_down: bfloat16 [16, 768, 2048], P('req', 'tp'), may hold values from -0.21875 to 0.21875
- gain_out: float32 [2048], replicated, may hold values from 0.5 to 1.5
Outputs:
- normed: bfloat16 [1024, 2048], P(('req', 'tp'))
Inputs may be any that keep to these rules, and one draw needn't show every extreme that they name: `route_ids`: each row names 8 different experts; in each aligned block of 32 rows no expert is named by more than 32 rows, and in some block some expert by exactly 32. `expert_home`: each expert is held by exactly one group. `request_page_index`: entries number pages among the 4 pages of the request's own group; a page may be named by several requests and entries. `cache_length_rows`: in every group one request has exactly 512 cached tokens.
All inputs are finite; a program needn't handle non-finite values.
Results may differ from a plain program's by a relative error of at most 0.0058.
Values may be sent and summed in bfloat16 or wider, within the bound.
No kernel may reach another device: no remote copies, remote signals or barrier semaphores. Data moves between devices by JAX's collectives and lax.ppermute only.
A program may use at most 64 MiB of HBM per device.

v0:
```python
import jax
import jax.numpy as jnp
from jax import lax
from jax.sharding import PartitionSpec as P

HEAD_WIDTH = 128
TOPK = 8
PRE_DEV = 56
EPSILON = 1e-06


def rms_scale(value_rows, gain_row):
    mean_square = jnp.mean(value_rows * value_rows, axis=-1, keepdims=True)
    return value_rows * lax.rsqrt(mean_square + EPSILON) * gain_row


def softmax_rounded(scores):
    row_peak = jnp.max(scores, axis=-1, keepdims=True)
    weights = jnp.exp(scores - row_peak)
    return (weights / jnp.sum(weights, axis=-1, keepdims=True)).astype(jnp.bfloat16)


def group_attention(queries, fresh_key_value, page_pool, page_rows, lengths):
    tokens_here = queries.shape[0]
    kv_heads = fresh_key_value.shape[1] // (2 * HEAD_WIDTH)
    group_size = queries.shape[1] // (HEAD_WIDTH * kv_heads)
    score_scale = HEAD_WIDTH ** (-0.5)
    split_query = queries.reshape(tokens_here, kv_heads, group_size, HEAD_WIDTH)
    fresh_kv = fresh_key_value.reshape(tokens_here, kv_heads, 2, HEAD_WIDTH)
    gathered_pages = page_pool[page_rows]
    cached = gathered_pages.reshape(page_rows.shape[0], -1, kv_heads, 2, HEAD_WIDTH)
    places = jnp.arange(cached.shape[1], dtype=jnp.int32)
    prefill_query = split_query[:PRE_DEV]
    prefill_fresh = fresh_kv[:PRE_DEV]
    cache_scores = (
        jnp.einsum(
            "ikgd,ckd->kgic", prefill_query, cached[0, :, :, 0], preferred_element_type=jnp.float32
        )
        * score_scale
    )
    cache_scores = jnp.where(places < lengths[0], cache_scores, -jnp.inf)
    block_scores = (
        jnp.einsum(
            "ikgd,jkd->kgij",
            prefill_query,
            prefill_fresh[:, :, 0],
            preferred_element_type=jnp.float32,
        )
        * score_scale
    )
    causal = jnp.arange(PRE_DEV)[:, None] >= jnp.arange(PRE_DEV)[None, :]
    block_scores = jnp.where(causal, block_scores, -jnp.inf)
    prefill_probs = softmax_rounded(jnp.concatenate([cache_scores, block_scores], axis=3))
    prefill_values = jnp.concatenate([cached[0, :, :, 1], prefill_fresh[:, :, 1]], axis=0)
    prefill_out = jnp.einsum(
        "kgic,ckd->ikgd", prefill_probs, prefill_values, preferred_element_type=jnp.float32
    )
    decode_query = split_query[PRE_DEV:]
    decode_fresh = fresh_kv[PRE_DEV:]
    decode_scores = (
        jnp.einsum(
            "rkgd,rckd->rkgc", decode_query, cached[1:, :, :, 0], preferred_element_type=jnp.float32
        )
        * score_scale
    )
    decode_scores = jnp.where(
        places[None, None, None, :] < lengths[1:, None, None, None], decode_scores, -jnp.inf
    )
    own_scores = (
        jnp.einsum(
            "rkgd,rkd->rkg", decode_query, decode_fresh[:, :, 0], preferred_element_type=jnp.float32
        )[..., None]
        * score_scale
    )
    decode_probs = softmax_rounded(jnp.concatenate([decode_scores, own_scores], axis=3))
    decode_values = jnp.concatenate([cached[1:, :, :, 1], decode_fresh[:, None, :, 1]], axis=1)
    decode_out = jnp.einsum(
        "rkgc,rckd->rkgd", decode_probs, decode_values, preferred_element_type=jnp.float32
    )
    joined = jnp.concatenate([prefill_out, decode_out], axis=0)
    return joined.reshape(tokens_here, -1).astype(jnp.bfloat16)


def slot_positions(block_owner, experts, capacity):
    flat_owner = block_owner.reshape(-1)
    onehot = (flat_owner[:, None] == jnp.arange(experts, dtype=jnp.int32)[None, :]).astype(
        jnp.int32
    )
    earlier = jnp.cumsum(onehot, axis=0) - onehot
    slot_index = jnp.sum(earlier * onehot, axis=1)
    return (flat_owner * capacity + slot_index).reshape(block_owner.shape)


def place_matrix(positions, slots_total):
    matches = positions[None, :, :] == jnp.arange(slots_total, dtype=jnp.int32)[:, None, None]
    return jnp.any(matches, axis=2).astype(jnp.bfloat16)


def local(
    queries,
    fresh_key_value,
    key_value_cache,
    request_page_index,
    cache_length_rows,
    residual,
    w_out,
    gain_in,
    route_ids,
    route_weights,
    expert_home,
    w_gate,
    w_up,
    w_down,
    gain_out,
):
    tp_size = lax.axis_size("tp")
    req_size = lax.axis_size("req")
    tp_index = lax.axis_index("tp")
    model_width = residual.shape[1]
    tokens_here = residual.shape[0]
    quarter = tokens_here // tp_size
    experts = expert_home.shape[0]
    capacity = min(quarter, max(2, 2 * quarter * TOPK // experts))
    context = group_attention(
        queries, fresh_key_value, key_value_cache, request_page_index, cache_length_rows
    )
    head_terms = jnp.dot(context, w_out, preferred_element_type=jnp.float32)
    state = residual.astype(jnp.float32) + lax.psum(head_terms, "tp")
    owners = jnp.sum(
        jnp.where(
            route_ids[:, :, None] == jnp.arange(experts, dtype=jnp.int32)[None, None, :],
            expert_home[None, None, :],
            0,
        ),
        axis=2,
    )
    shares = route_weights / jnp.sum(route_weights, axis=1, keepdims=True)
    own_start = tp_index * quarter
    own_state = lax.dynamic_slice_in_dim(state, own_start, quarter, 0)
    own_shares = lax.dynamic_slice_in_dim(shares, own_start, quarter, 0)
    normed_all = rms_scale(state, gain_in).astype(jnp.bfloat16)
    positions_all = jax.vmap(lambda block_owner: slot_positions(block_owner, experts, capacity))(
        owners.reshape(tp_size, quarter, TOPK)
    )
    placing = jax.vmap(lambda positions: place_matrix(positions, experts * capacity))(positions_all)
    outgoing = jnp.einsum(
        "qmi,qid->qmd",
        placing,
        normed_all.reshape(tp_size, quarter, model_width),
        preferred_element_type=jnp.float32,
    )
    outgoing = outgoing.astype(jnp.bfloat16).reshape(tp_size, experts, capacity, model_width)
    incoming = lax.all_to_all(outgoing, "req", split_axis=1, concat_axis=1, tiled=True)
    own_positions = lax.dynamic_index_in_dim(positions_all, tp_index, 0, keepdims=False)
    expert_rows = incoming.reshape(-1, model_width)
    gate_proj = jnp.dot(expert_rows, w_gate[0], preferred_element_type=jnp.float32)
    up_proj = jnp.dot(expert_rows, w_up[0], preferred_element_type=jnp.float32)
    inner_units = (jax.nn.silu(gate_proj) * up_proj).astype(jnp.bfloat16)
    summed = lax.psum_scatter(
        jnp.dot(inner_units, w_down[0], preferred_element_type=jnp.float32).astype(jnp.bfloat16),
        "tp",
        scatter_dimension=0,
        tiled=True,
    )
    results = summed.reshape(req_size, capacity, model_width)
    returned = lax.all_to_all(results, "req", split_axis=0, concat_axis=0, tiled=True).reshape(
        -1, model_width
    )
    picked = returned[own_positions]
    mixture = jnp.sum(own_shares[:, :, None] * picked.astype(jnp.float32), axis=1)
    return rms_scale(own_state + mixture, gain_out).astype(jnp.bfloat16)


def solution(mesh):
    return jax.shard_map(
        local,
        mesh=mesh,
        in_specs=(
            P("req", "tp"),
            P("req", "tp"),
            P("req", None, "tp"),
            P("req", None),
            P("req"),
            P("req", None),
            P("tp", None),
            P(),
            P("req", None),
            P("req", None),
            P(),
            P("req", None, "tp"),
            P("req", None, "tp"),
            P("req", "tp", None),
            P(),
        ),
        out_specs=P(("req", "tp"), None),
        check_vma=False,
    )
```

profile of v0, /device:TPU:13, one launch (start us, length us, event | category | flops | bytes accessed | tf_op | source)
XLA Modules:
  0.0 313.9 jit_solution(11618750523219073472)
XLA Ops:
  6.5 0.8 compare_select_fusion.1
  7.3 0.1 copy.76
  7.5 5.4 %gather_fusion = bf16[36,128,512]{2,1,0:T(8,128)(2,1)} fusion(bf16[4,128,512]{2,1,0:T(8,128)(2,1)} %param.17, s32[1024]{0:T(1024)S(1)} %pad_clamp_fusion.1), kind=kCustom, calls=%fused_computation | custom fusion | bytes 9437328 | tf_op jit(solution)/shard_map/gather | solution.py:30
  13.0 7.7 %reshape.139 = bf16[9,512,2,2,128]{4,3,2,1,0:T(2,128)(2,1)} reshape(bf16[36,128,512]{2,1,0:T(8,128)(2,1)} %gather_fusion) | data formatting | bytes 9437184 | tf_op jit(solution)/shard_map/reshape | solution.py:31
  20.7 10.0 %fusion.46 = (bf16[8,512,2,1,128]{4,3,2,1,0:T(2,128)(2,1)}, bf16[8,512,2,1,128]{4,3,2,1,0:T(2,128)(2,1)}) fusion(bf16[9,512,2,2,128]{4,3,2,1,0:T(2,128)(2,1)} %reshape.139), kind=kLoop, calls=%fused_computation.93 | loop fusion | bytes 8388608 | tf_op jit(solution)/shard_map/slice | solution.py:62
  30.7 2.1 fusion.45
  33.1 0.1 fusion.38
  33.2 2.9 fusion.48
  36.2 0.2 copy.85
  36.4 2.7 copy.146
  39.1 0.2 fusion.33
  39.4 0.5 fusion
  39.9 0.4 slice-done.1
  40.4 0.1 fusion.47
  40.5 0.4 fusion.49
  40.9 0.3 fusion.50
  41.3 0.3 fusion.23
  41.6 0.5 fusion.21
  42.1 0.1 copy.89
  42.3 3.9 %fusion.51 = f32[64,2048]{1,0:T(8,128)} fusion(bf16[64,1024]{1,0:T(8,128)(2,1)S(1)} %convert_element_type.42, bf16[1024,2048]{1,0:T(8,128)(2,1)} %param.21), kind=kOutput, calls=%fused_computation.98 | convolution fusion | flops 268435456 | bytes 4849664 | tf_op jit(solution)/shard_map/dot_general | solution.py:127
  46.3 0.1 select_reduce_fusion
  46.4 0.1 copy.91
  46.5 0.1 eq.58
  46.6 1.2 reduce-window.6
  47.7 0.2 slice_reduce_fusion
  47.9 0.1 eq.54
  48.1 0.1 fusion.36
  48.2 0.1 reduce_sum.79
  48.3 0.1 copy.104
  48.4 0.4 fusion.22
  48.8 27.4 %all-reduce.2.cloned.1.call-done = f32[64,2048]{1,0:T(8,128)} async-done(((f32[64,2048]{1,0:T(8,128)}), f32[64,2048]{1,0:T(8,128)}) %all-reduce.2.cloned.1.call-update) | async-done | bytes 524304 | tf_op jit(solution)/shard_map/psum | solution.py:128
  76.1 1.2 multiply_reduce_fusion
  77.4 0.1 multiply_convert_fusion.1
  77.5 1.3 convolution_convert_fusion.1
  78.8 0.6 copy.95
  79.4 98.4 %all_to_all.10 = bf16[2,16,32,2048]{3,2,0,1:T(8,128)(2,1)S(1)} all-to-all(bf16[2,16,32,2048]{3,2,0,1:T(8,128)(2,1)S(1)} %copy.95), channel_id=1, replica_groups=mesh['req'=16,'tp'=2] {'req'}, dimensions={1} | all-to-all | bytes 8388608 | tf_op jit(solution)/shard_map/all_to_all | solution.py:153
  177.8 0.6 copy.96
  178.4 2.0 copy-done.1
  180.3 3.6 %fusion.9 = f32[1024,384]{1,0:T(8,128)} fusion(bf16[1024,2048]{1,0:T(8,128)(2,1)S(1)} %bitcast.118, bf16[1,2048,384]{2,1,0:T(8,128)(2,1)S(1)} %copy-done.8), kind=kOutput, calls=%fused_computation.16 | convolution fusion | flops 1610612736 | bytes 7340032 | tf_op jit(solution)/shard_map/dot_general | solution.py:156
  183.9 9.6 %convolution_convert_fusion = bf16[1024,2048]{1,0:T(8,128)(2,1)} fusion(bf16[1,384,2048]{2,1,0:T(8,128)(2,1)S(1)} %copy-done, f32[1024,384]{1,0:T(8,128)} %fusion.9, bf16[1024,2048]{1,0:T(8,128)(2,1)} %bitcast.119, bf16[1,2048,384]{2,1,0:T(8,128)(2,1)} %param.27), kind=kOutput, calls=%fused_computation.2 | convolution fusion | flops 3225681920 | bytes 13107200 | tf_op jit(solution)/shard_map/dot_general | solution.py:160
  193.5 53.4 %reduce-scatter.2.cloned.1.call-done = bf16[512,2048]{1,0:T(8,128)(2,1)} async-done(((bf16[1024,2048]{1,0:T(8,128)(2,1)}), bf16[512,2048]{1,0:T(8,128)(2,1)}) %reduce-scatter.2.cloned.1.call-update) | async-done | bytes 2097168 | tf_op jit(solution)/shard_map/reduce_scatter | solution.py:159
  246.9 6.5 %all-to-all-start.1 = ((bf16[16,32,2048]{2,1,0:T(8,128)(2,1)}), bf16[16,32,2048]{2,1,0:T(8,128)(2,1)}, u32[]{:S(2)}, u32[]{:S(2)}) async-start(bf16[16,32,2048]{2,1,0:T(8,128)(2,1)} %bitcast.121), calls=%async_computation.2 | async-start | bytes 4194304 | tf_op jit(solution)/shard_map/all_to_all | solution.py:166
  253.4 0.1 reshape.156
  253.7 47.2 %all-to-all-done.1 = bf16[16,32,2048]{2,1,0:T(8,128)(2,1)} async-done(((bf16[16,32,2048]{2,1,0:T(8,128)(2,1)}), bf16[16,32,2048]{2,1,0:T(8,128)(2,1)}, u32[]{:S(2)}, u32[]{:S(2)}) %all-to-all-start.1) | async-done | bytes 2097184 | tf_op jit(solution)/shard_map/all_to_all | solution.py:166
  300.9 4.2 %gather_fusion.1 = bf16[256,2048]{1,0:T(8,128)(2,1)S(1)} fusion(bf16[512,2048]{1,0:T(8,128)(2,1)} %bitcast.33, s32[1024]{0:T(1024)S(1)} %pad_clamp_fusion), kind=kCustom, calls=%fused_computation.1 | custom fusion | bytes 2098176 | tf_op jit(solution)/shard_map/gather | solution.py:169
  305.2 1.0 fusion.5
  306.2 0.2 multiply_reduce_fusion.1
  306.3 0.8 multiply_convert_fusion.2
  (61 shorter events, 1.0 us)
Async XLA Ops:
  6.5 177.4 %copy-start = (bf16[1,384,2048]{2,1,0:T(8,128)(2,1)S(1)}, bf16[1,384,2048]{2,1,0:T(8,128)(2,1)}, u32[]{:S(2)}) copy-start(bf16[1,384,2048]{2,1,0:T(8,128)(2,1)} %param.28) | copy-start | bytes 4718596
  6.5 69.6 %all-reduce.2.cloned.1.call-start = ((), (), s32[]{:S(2)}) async-start(), calls=%async_computation.3 | async-start | bytes 1048576 | tf_op jit(solution)/shard_map/psum | solution.py:128
  30.7 2.2 slice-start
  30.7 2.2 copy-start.9
  30.7 2.3 slice-start.2
  39.3 0.9 slice-start.1
  39.3 1.0 slice-start.3
  42.3 4.0 %copy-start.6 = (s32[64,8]{0,1:T(8,128)S(1)}, s32[64,8]{0,1:T(8,128)}, u32[]{:S(2)}) copy-start(s32[64,8]{0,1:T(8,128)} %param.23) | copy-start | bytes 6148
  42.3 4.0 %copy-start.7 = (s32[16]{0:T(128)S(1)}, s32[16]{0:T(128)}, u32[]{:S(2)}) copy-start(s32[16]{0:T(128)} %param.25) | copy-start | bytes 196
  42.3 33.8 %copy-start.2 = (bf16[64,2048]{1,0:T(8,128)(2,1)S(1)}, bf16[64,2048]{1,0:T(8,128)(2,1)}, u32[]{:S(2)}) copy-start(bf16[64,2048]{1,0:T(8,128)(2,1)} %param.20) | copy-start | bytes 786436
  46.2 31.2 %copy-start.4 = (f32[2048]{0:T(1024)S(1)}, f32[2048]{0:T(1024)}, u32[]{:S(2)}) copy-start(f32[2048]{0:T(1024)} %param.22) | copy-start | bytes 24580
  46.2 200.7 %reduce-scatter.2.cloned.1.call-start = ((), (), s32[]{:S(2)}) async-start(), calls=%async_computation.4 | async-start | bytes 6291456 | tf_op jit(solution)/shard_map/reduce_scatter | solution.py:159
  177.8 2.6 copy-start.8
  178.4 2.0 copy-start.1
  246.9 6.6 %copy-start.3 = (f32[64,8]{0,1:T(8,128)S(1)}, f32[64,8]{0,1:T(8,128)}, u32[]{:S(2)}) copy-start(f32[64,8]{0,1:T(8,128)} %param.24) | copy-start | bytes 6148
  246.9 54.0 %all-to-all-start.1 = ((bf16[16,32,2048]{2,1,0:T(8,128)(2,1)}), bf16[16,32,2048]{2,1,0:T(8,128)(2,1)}, u32[]{:S(2)}, u32[]{:S(2)}) async-start(bf16[16,32,2048]{2,1,0:T(8,128)(2,1)} %bitcast.121), calls=%async_computation.2 | async-start | bytes 4194304 | tf_op jit(solution)/shard_map/all_to_all | solution.py:166
  300.9 5.4 %copy-start.5 = (f32[2048]{0:T(1024)S(1)}, f32[2048]{0:T(1024)}, u32[]{:S(2)}) copy-start(f32[2048]{0:T(1024)} %param.29) | copy-start | bytes 24580
Sparse Core Ops, SparseCore 0:
  46.3 29.7 all-reduce.1
  193.6 53.2 reduce-scatter.1
where the time goes:
time: 315 us; the launch traced here: 314 us
  waiting for transfers between devices  128 us (41%)
  blocking collectives  98.4 us (31%)
  local copies, waits for them, and re-layouts  37.6 us (12%)
  matrix products  23 us (7%)
  between operations  13.8 us (4%)
  starting transfers between devices  6.55 us (2%)
  other arithmetic  6.54 us (2%)
    all_to_all x1, blocking collectives, local(): lax.all_to_all(outgoing, 'req', split_axis=1, concat_axis=1, tiled=True)  98.4 us
    reduce_scatter x1, waiting for transfers between devices, local(): lax.psum_scatter(jnp.dot(inner_units, w_down[0], preferred_element_type=j...  53.4 us
    all_to_all x1, waiting for transfers between devices, local(): lax.all_to_all(results, 'req', split_axis=0, concat_axis=0, tiled=True)  47.2 us
    psum x1, waiting for transfers between devices, local(): state = residual.astype(jnp.float32) + lax.psum(head_terms, 'tp')  27.4 us
    slice x1, local copies, waits for them, and re-layouts, group_attention(): cached[1:, :, :, 0]  10 us
    dot_general x1, matrix products, local(): jnp.dot(inner_units, w_down[0], preferred_element_type=jnp.float32)  9.56 us
    reshape x1, local copies, waits for them, and re-layouts, group_attention(): gathered_pages.reshape(page_rows.shape[0], -1, kv_heads, 2, HEAD_WIDTH)  7.7 us
    all_to_all x1, starting transfers between devices, local(): lax.all_to_all(results, 'req', split_axis=0, concat_axis=0, tiled=True)  6.5 us
  transfers between devices with their start and end apart: 3, of which 3 were waited for; matrix products, arithmetic and copies ran while one was open for 1% of the time, Pallas kernels for 0%

commit v1 on v0

--- a/solution.py
+++ b/solution.py
@@ -7,6 +7,29 @@
 TOPK = 8
 PRE_DEV = 56
 EPSILON = 1e-06
+
+
+def in_blocks(x, dim, peers):
+    shape = x.shape
+    blocks = x.reshape(*shape[:dim], peers, shape[dim] // peers, *shape[dim + 1 :])
+    return jnp.moveaxis(blocks, dim, 0)
+
+
+def joined_along(parts, dim):
+    dims = list(parts.shape[1:])
+    dims[dim] *= parts.shape[0]
+    return jnp.moveaxis(parts, 0, dim).reshape(dims)
+
+
+def pairwise_exchange(x, axis, split_dim, concat_dim):
+    size, here = (lax.axis_size(axis), lax.axis_index(axis))
+    tiles = in_blocks(x, split_dim, size)
+    outs = [tiles[here]]
+    for step in range(1, size):
+        sent = tiles[here ^ step]
+        outs.append(lax.ppermute(sent, axis, [(i, i ^ step) for i in range(size)]))
+    tiles = jnp.stack(outs)[here ^ jnp.arange(size)]
+    return joined_along(tiles, concat_dim)
 
 
 def rms_scale(value_rows, gain_row):
@@ -163,9 +186,7 @@
         tiled=True,
     )
     results = summed.reshape(req_size, capacity, model_width)
-    returned = lax.all_to_all(results, "req", split_axis=0, concat_axis=0, tiled=True).reshape(
-        -1, model_width
-    )
+    returned = pairwise_exchange(results, "req", 0, 0).reshape(-1, model_width)
     picked = returned[own_positions]
     mixture = jnp.sum(own_shares[:, :, None] * picked.astype(jnp.float32), axis=1)
     return rms_scale(own_state + mixture, gain_out).astype(jnp.bfloat16)

time: 315 us -> 328 us (1.041)
  waiting for transfers between devices: 128 us -> 110 us
  local copies, waits for them, and re-layouts: 37.6 us -> 54.6 us
  starting transfers between devices: 6.55 us -> 19.5 us
    all_to_all x1 -> x0, waiting for transfers between devices: 47.2 us -> none  [local(): lax.all_to_all(results, 'req', split_axis=0, concat_axis=0, tiled=True)]
    ppermute x0 -> x15, waiting for transfers between devices: none -> 27.5 us  [pairwise_exchange(): outs.append(lax.ppermute(sent, axis, [(i, i ^ step) for i in range(size)]))]
    ppermute x0 -> x15, starting transfers between devices: none -> 19.5 us  [pairwise_exchange(): outs.append(lax.ppermute(sent, axis, [(i, i ^ step) for i in range(size)]))]
    unnamed x23 -> x37, local copies, waits for them, and re-layouts: 4.77 us -> 15.4 us
    all_to_all x1 -> x0, starting transfers between devices: 6.5 us -> none  [local(): lax.all_to_all(results, 'req', split_axis=0, concat_axis=0, tiled=True)]
    gather x0 -> x1, local copies, waits for them, and re-layouts: none -> 3.56 us  [pairwise_exchange(): tiles = jnp.stack(outs)[here ^ jnp.arange(size)]]
  transfers between devices with their start and end apart: 3 -> 17, of which waited for: 3 -> 10; matrix products, arithmetic and copies ran while one was open for 1% -> 3% of each run, Pallas kernels for 0% -> 0%
where the time goes in v1:
time: 328 us; the launch traced here: 326 us
  waiting for transfers between devices  110 us (34%)
  blocking collectives  98.4 us (30%)
  local copies, waits for them, and re-layouts  54.6 us (17%)
  matrix products  23 us (7%)
  starting transfers between devices  19.5 us (6%)
  between operations  13.9 us (4%)
  other arithmetic  7.29 us (2%)
    all_to_all x1, blocking collectives, local(): lax.all_to_all(outgoing, 'req', split_axis=1, concat_axis=1, tiled=True)  98.4 us
    reduce_scatter x1, waiting for transfers between devices, local(): lax.psum_scatter(jnp.dot(inner_units, w_down[0], preferred_element_type=j...  52.6 us
    psum x1, waiting for transfers between devices, local(): state = residual.astype(jnp.float32) + lax.psum(head_terms, 'tp')  29.4 us
    ppermute x15, waiting for transfers between devices, pairwise_exchange(): outs.append(lax.ppermute(sent, axis, [(i, i ^ step) for i in range(size)]))  27.5 us
    ppermute x15, starting transfers between devices, pairwise_exchange(): outs.append(lax.ppermute(sent, axis, [(i, i ^ step) for i in range(size)]))  19.5 us
    unnamed x37, local copies, waits for them, and re-layouts  15.4 us
    slice x1, local copies, waits for them, and re-layouts, group_attention(): cached[1:, :, :, 0]  10 us
    dot_general x1, matrix products, local(): jnp.dot(inner_units, w_down[0], preferred_element_type=jnp.float32)  9.56 us
  transfers between devices with their start and end apart: 17, of which 10 were waited for; matrix products, arithmetic and copies ran while one was open for 3% of the time, Pallas kernels for 0%

profile of v1, /device:TPU:13, one launch (start us, length us, event | category | flops | bytes accessed | tf_op | source)
XLA Modules:
  0.0 326.2 jit_solution(6025311248421793141)
XLA Ops:
  6.5 0.9 select_reduce_fusion
  7.8 1.2 reduce-window.6
  9.6 0.7 compare_select_fusion.1
  10.5 4.4 %gather_fusion = bf16[36,128,512]{2,1,0:T(8,128)(2,1)} fusion(bf16[4,128,512]{2,1,0:T(8,128)(2,1)S(1)} %copy-done.1, s32[1024]{0:T(1024)S(1)} %get-tuple-element.40), kind=kCustom, calls=%fused_computation | custom fusion | bytes 9437328 | tf_op jit(solution)/shard_map/gather | solution.py:53
  14.9 7.7 %reshape.149 = bf16[9,512,2,2,128]{4,3,2,1,0:T(2,128)(2,1)} reshape(bf16[36,128,512]{2,1,0:T(8,128)(2,1)} %gather_fusion) | data formatting | bytes 9437184 | tf_op jit(solution)/shard_map/reshape | solution.py:54
  22.6 10.0 %fusion.47 = (bf16[8,512,2,1,128]{4,3,2,1,0:T(2,128)(2,1)}, bf16[8,512,2,1,128]{4,3,2,1,0:T(2,128)(2,1)}) fusion(bf16[9,512,2,2,128]{4,3,2,1,0:T(2,128)(2,1)} %reshape.149), kind=kLoop, calls=%fused_computation.128 | loop fusion | bytes 8388608 | tf_op jit(solution)/shard_map/slice | solution.py:85
  32.7 2.1 fusion.46
  35.1 2.9 fusion.49
  38.3 2.7 copy.146
  44.2 3.9 %fusion.52 = f32[64,2048]{1,0:T(8,128)} fusion(bf16[64,1024]{1,0:T(8,128)(2,1)S(1)} %convert_element_type.42, bf16[1024,2048]{1,0:T(8,128)(2,1)} %param.21), kind=kOutput, calls=%fused_computation.133 | convolution fusion | flops 268435456 | bytes 4849664 | tf_op jit(solution)/shard_map/dot_general | solution.py:150
  48.5 29.4 %all-reduce.2.cloned.1.call-done = f32[64,2048]{1,0:T(8,128)} async-done(((f32[64,2048]{1,0:T(8,128)}), f32[64,2048]{1,0:T(8,128)}) %all-reduce.2.cloned.1.call-update) | async-done | bytes 524304 | tf_op jit(solution)/shard_map/psum | solution.py:151
  78.0 1.2 multiply_reduce_fusion
  79.3 1.3 convolution_convert_fusion.1
  81.2 98.4 %all_to_all.5 = bf16[2,16,32,2048]{3,2,0,1:T(8,128)(2,1)S(1)} all-to-all(bf16[2,16,32,2048]{3,2,0,1:T(8,128)(2,1)S(1)} %copy.95), channel_id=1, replica_groups=mesh['req'=16,'tp'=2] {'req'}, dimensions={1} | all-to-all | bytes 8388608 | tf_op jit(solution)/shard_map/all_to_all | solution.py:176
  180.2 2.0 copy-done.2
  182.2 3.6 %fusion.9 = f32[1024,384]{1,0:T(8,128)} fusion(bf16[1024,2048]{1,0:T(8,128)(2,1)S(1)} %bitcast.182, bf16[1,2048,384]{2,1,0:T(8,128)(2,1)S(1)} %copy-done.8), kind=kOutput, calls=%fused_computation.17 | convolution fusion | flops 1610612736 | bytes 7340032 | tf_op jit(solution)/shard_map/dot_general | solution.py:179
  185.7 9.6 %convolution_convert_fusion = bf16[1024,2048]{1,0:T(8,128)(2,1)} fusion(bf16[1,384,2048]{2,1,0:T(8,128)(2,1)S(1)} %copy-done, f32[1024,384]{1,0:T(8,128)} %fusion.9, bf16[1024,2048]{1,0:T(8,128)(2,1)} %bitcast.183, bf16[1,2048,384]{2,1,0:T(8,128)(2,1)} %param.27), kind=kOutput, calls=%fused_computation.3 | convolution fusion | flops 3225681920 | bytes 13107200 | tf_op jit(solution)/shard_map/dot_general | solution.py:183
  196.1 52.6 %reduce-scatter.2.cloned.1.call-done = bf16[512,2048]{1,0:T(8,128)(2,1)} async-done(((bf16[1024,2048]{1,0:T(8,128)(2,1)}), bf16[512,2048]{1,0:T(8,128)(2,1)}) %reduce-scatter.2.cloned.1.call-update) | async-done | bytes 2097168 | tf_op jit(solution)/shard_map/reduce_scatter | solution.py:182
  248.7 2.5 dynamic-slice_bitcast_fusion
  251.2 0.7 collective-permute-start
  251.9 0.7 copy.90
  252.8 1.4 collective-permute-start.2
  254.5 1.6 collective-permute-start.4
  256.3 1.6 bitcast_dynamic-update-slice_fusion.14
  257.9 2.3 collective-permute-start.6
  260.2 0.7 bitcast_dynamic-update-slice_fusion.13
  261.1 2.1 collective-permute-start.7
  263.2 0.7 bitcast_dynamic-update-slice_fusion.12
  264.3 0.7 bitcast_dynamic-update-slice_fusion.11
  265.0 2.1 collective-permute-start.9
  267.7 5.5 %collective-permute-start.10 = (bf16[1,32,2048]{2,1,0:T(8,128)(2,1)S(1)}, bf16[1,32,2048]{2,1,0:T(8,128)(2,1)S(1)}, u32[]{:S(2)}, u32[]{:S(2)}) collective-permute-start(bf16[1,32,2048]{2,1,0:T(8,128)(2,1)S(1)} %get-tuple-element.15), channel_id=1, source_target_pairs={{0,22},{2,20},{4,18},{6,16},{8,30},{10,28},{12,26},{14,24},{16,6},... | collective-permute-start | bytes 393224 | tf_op jit(solution)/shard_map/ppermute | solution.py:30
  273.8 1.1 collective-permute-start.11
  275.0 0.7 bitcast_dynamic-update-slice_fusion.8
  276.3 9.6 %collective-permute-done.8 = bf16[1,32,2048]{2,1,0:T(8,128)(2,1)S(1)} collective-permute-done((bf16[1,32,2048]{2,1,0:T(8,128)(2,1)S(1)}, bf16[1,32,2048]{2,1,0:T(8,128)(2,1)S(1)}, u32[]{:S(2)}, u32[]{:S(2)}) %collective-permute-start.8) | collective-permute-done | bytes 131104 | tf_op jit(solution)/shard_map/ppermute | solution.py:30
  285.9 0.7 bitcast_dynamic-update-slice_fusion.6
  286.6 2.1 collective-permute-done.9
  288.7 1.5 collective-permute-start.14
  290.9 3.3 %collective-permute-done.10 = bf16[1,32,2048]{2,1,0:T(8,128)(2,1)S(1)} collective-permute-done((bf16[1,32,2048]{2,1,0:T(8,128)(2,1)S(1)}, bf16[1,32,2048]{2,1,0:T(8,128)(2,1)S(1)}, u32[]{:S(2)}, u32[]{:S(2)}) %collective-permute-start.10) | collective-permute-done | bytes 131104 | tf_op jit(solution)/shard_map/ppermute | solution.py:30
  294.2 0.7 bitcast_dynamic-update-slice_fusion.4
  294.8 5.3 %collective-permute-done.11 = bf16[1,32,2048]{2,1,0:T(8,128)(2,1)S(1)} collective-permute-done((bf16[1,32,2048]{2,1,0:T(8,128)(2,1)S(1)}, bf16[1,32,2048]{2,1,0:T(8,128)(2,1)S(1)}, u32[]{:S(2)}, u32[]{:S(2)}) %collective-permute-start.11) | collective-permute-done | bytes 131104 | tf_op jit(solution)/shard_map/ppermute | solution.py:30
  300.8 2.5 collective-permute-done.12
  304.0 1.7 collective-permute-done.13
  306.3 2.6 collective-permute-done.14
  308.9 0.7 bitcast_dynamic-update-slice_fusion
  309.6 3.6 %gather_fusion.1 = bf16[16,32,2048]{2,1,0:T(8,128)(2,1)} fusion(bf16[16,32,2048]{2,1,0:T(8,128)(2,1)} %bitcast.184, s32[1024]{0:T(1024)S(1)} %pad_clamp_fusion.1), kind=kCustom, calls=%fused_computation.1 | custom fusion | bytes 4194368 | tf_op jit(solution)/shard_map/gather | solution.py:31
  313.2 4.2 %gather_fusion.2 = bf16[256,2048]{1,0:T(8,128)(2,1)S(1)} fusion(bf16[512,2048]{1,0:T(8,128)(2,1)} %bitcast.180, s32[1024]{0:T(1024)S(1)} %get-tuple-element.39), kind=kCustom, calls=%fused_computation.2 | custom fusion | bytes 2098176 | tf_op jit(solution)/shard_map/gather | solution.py:190
  317.4 1.0 fusion.5
  318.6 0.8 multiply_convert_fusion.2
  (107 shorter events, 13.3 us)
Async XLA Ops:
  6.5 179.2 %copy-start = (bf16[1,384,2048]{2,1,0:T(8,128)(2,1)S(1)}, bf16[1,384,2048]{2,1,0:T(8,128)(2,1)}, u32[]{:S(2)}) copy-start(bf16[1,384,2048]{2,1,0:T(8,128)(2,1)} %param.28) | copy-start | bytes 4718596
  6.5 3.9 %copy-start.1 = (bf16[4,128,512]{2,1,0:T(8,128)(2,1)S(1)}, bf16[4,128,512]{2,1,0:T(8,128)(2,1)}, u32[]{:S(2)}) copy-start(bf16[4,128,512]{2,1,0:T(8,128)(2,1)} %param.17) | copy-start | bytes 1572868
  6.5 71.4 %all-reduce.2.cloned.1.call-start = ((), (), s32[]{:S(2)}) async-start(), calls=%async_computation.2 | async-start | bytes 1048576 | tf_op jit(solution)/shard_map/psum | solution.py:151
  32.6 2.2 slice-start
  32.6 2.2 copy-start.9
  32.6 2.3 slice-start.2
  41.2 0.9 slice-start.1
  41.3 1.0 slice-start.3
  44.2 33.8 %copy-start.3 = (bf16[64,2048]{1,0:T(8,128)(2,1)S(1)}, bf16[64,2048]{1,0:T(8,128)(2,1)}, u32[]{:S(2)}) copy-start(bf16[64,2048]{1,0:T(8,128)(2,1)} %param.20) | copy-start | bytes 786436
  44.2 35.0 %copy-start.6 = (f32[2048]{0:T(1024)S(1)}, f32[2048]{0:T(1024)}, u32[]{:S(2)}) copy-start(f32[2048]{0:T(1024)} %param.22) | copy-start | bytes 24580
  48.1 200.6 %reduce-scatter.2.cloned.1.call-start = ((), (), s32[]{:S(2)}) async-start(), calls=%async_computation.3 | async-start | bytes 6291456 | tf_op jit(solution)/shard_map/reduce_scatter | solution.py:182
  179.6 2.6 copy-start.8
  180.2 2.0 copy-start.2
  195.3 0.7 copy-start.5
  251.2 4.9 %collective-permute-start = (bf16[1,32,2048]{2,1,0:T(8,128)(2,1)}, bf16[1,32,2048]{2,1,0:T(8,128)(2,1)}, u32[]{:S(2)}, u32[]{:S(2)}) collective-permute-start(bf16[1,32,2048]{2,1,0:T(8,128)(2,1)} %get-tuple-element.25), channel_id=1, source_target_pairs={{0,2},{2,0},{4,6},{6,4},{8,10},{10,8},{12,14},{14,12},{16,18},{18,... | collective-permute-start | bytes 393224 | tf_op jit(solution)/shard_map/ppermute | solution.py:30
  252.6 5.3 %collective-permute-start.1 = (bf16[1,32,2048]{2,1,0:T(8,128)(2,1)}, bf16[1,32,2048]{2,1,0:T(8,128)(2,1)S(1)}, u32[]{:S(2)}, u32[]{:S(2)}) collective-permute-start(bf16[1,32,2048]{2,1,0:T(8,128)(2,1)} %get-tuple-element.24), channel_id=1, source_target_pairs={{0,4},{2,6},{4,0},{6,2},{8,12},{10,14},{12,8},{14,10},{16,20},{18,... | collective-permute-start | bytes 393224 | tf_op jit(solution)/shard_map/ppermute | solution.py:30
  252.8 8.3 %collective-permute-start.2 = (bf16[1,32,2048]{2,1,0:T(8,128)(2,1)}, bf16[1,32,2048]{2,1,0:T(8,128)(2,1)S(1)}, u32[]{:S(2)}, u32[]{:S(2)}) collective-permute-start(bf16[1,32,2048]{2,1,0:T(8,128)(2,1)} %get-tuple-element.23), channel_id=1, source_target_pairs={{0,6},{2,4},{4,2},{6,0},{8,14},{10,12},{12,10},{14,8},{16,22},{18,... | collective-permute-start | bytes 393224 | tf_op jit(solution)/shard_map/ppermute | solution.py:30
  254.2 9.7 %collective-permute-start.3 = (bf16[1,32,2048]{2,1,0:T(8,128)(2,1)}, bf16[1,32,2048]{2,1,0:T(8,128)(2,1)S(1)}, u32[]{:S(2)}, u32[]{:S(2)}) collective-permute-start(bf16[1,32,2048]{2,1,0:T(8,128)(2,1)} %get-tuple-element.22), channel_id=1, source_target_pairs={{0,8},{2,10},{4,12},{6,14},{8,0},{10,2},{12,4},{14,6},{16,24},{18,... | collective-permute-start | bytes 393224 | tf_op jit(solution)/shard_map/ppermute | solution.py:30
  254.5 10.5 %collective-permute-start.4 = (bf16[1,32,2048]{2,1,0:T(8,128)(2,1)S(1)}, bf16[1,32,2048]{2,1,0:T(8,128)(2,1)S(1)}, u32[]{:S(2)}, u32[]{:S(2)}) collective-permute-start(bf16[1,32,2048]{2,1,0:T(8,128)(2,1)S(1)} %get-tuple-element.21), channel_id=1, source_target_pairs={{0,10},{2,8},{4,14},{6,12},{8,2},{10,0},{12,6},{14,4},{16,26},{18,... | collective-permute-start | bytes 393224 | tf_op jit(solution)/shard_map/ppermute | solution.py:30
  256.1 11.6 %collective-permute-start.5 = (bf16[1,32,2048]{2,1,0:T(8,128)(2,1)S(1)}, bf16[1,32,2048]{2,1,0:T(8,128)(2,1)S(1)}, u32[]{:S(2)}, u32[]{:S(2)}) collective-permute-start(bf16[1,32,2048]{2,1,0:T(8,128)(2,1)S(1)} %get-tuple-element.20), channel_id=1, source_target_pairs={{0,12},{2,14},{4,8},{6,10},{8,4},{10,6},{12,0},{14,2},{16,28},{18,... | collective-permute-start | bytes 393224 | tf_op jit(solution)/shard_map/ppermute | solution.py:30
  257.9 15.9 %collective-permute-start.6 = (bf16[1,32,2048]{2,1,0:T(8,128)(2,1)S(1)}, bf16[1,32,2048]{2,1,0:T(8,128)(2,1)S(1)}, u32[]{:S(2)}, u32[]{:S(2)}) collective-permute-start(bf16[1,32,2048]{2,1,0:T(8,128)(2,1)S(1)} %get-tuple-element.19), channel_id=1, source_target_pairs={{0,14},{2,12},{4,10},{6,8},{8,6},{10,4},{12,2},{14,0},{16,30},{18,... | collective-permute-start | bytes 393224 | tf_op jit(solution)/shard_map/ppermute | solution.py:30
  261.1 14.5 %collective-permute-start.7 = (bf16[1,32,2048]{2,1,0:T(8,128)(2,1)S(1)}, bf16[1,32,2048]{2,1,0:T(8,128)(2,1)S(1)}, u32[]{:S(2)}, u32[]{:S(2)}) collective-permute-start(bf16[1,32,2048]{2,1,0:T(8,128)(2,1)S(1)} %get-tuple-element.18), channel_id=1, source_target_pairs={{0,16},{2,18},{4,20},{6,22},{8,24},{10,26},{12,28},{14,30},{16,0},... | collective-permute-start | bytes 393224 | tf_op jit(solution)/shard_map/ppermute | solution.py:30
  263.9 22.0 %collective-permute-start.8 = (bf16[1,32,2048]{2,1,0:T(8,128)(2,1)S(1)}, bf16[1,32,2048]{2,1,0:T(8,128)(2,1)S(1)}, u32[]{:S(2)}, u32[]{:S(2)}) collective-permute-start(bf16[1,32,2048]{2,1,0:T(8,128)(2,1)S(1)} %get-tuple-element.17), channel_id=1, source_target_pairs={{0,18},{2,16},{4,22},{6,20},{8,26},{10,24},{12,30},{14,28},{16,2},... | collective-permute-start | bytes 393224 | tf_op jit(solution)/shard_map/ppermute | solution.py:30
  265.0 23.7 %collective-permute-start.9 = (bf16[1,32,2048]{2,1,0:T(8,128)(2,1)S(1)}, bf16[1,32,2048]{2,1,0:T(8,128)(2,1)S(1)}, u32[]{:S(2)}, u32[]{:S(2)}) collective-permute-start(bf16[1,32,2048]{2,1,0:T(8,128)(2,1)S(1)} %get-tuple-element.16), channel_id=1, source_target_pairs={{0,20},{2,22},{4,16},{6,18},{8,28},{10,30},{12,24},{14,26},{16,4},... | collective-permute-start | bytes 393224 | tf_op jit(solution)/shard_map/ppermute | solution.py:30
  267.7 26.5 %collective-permute-start.10 = (bf16[1,32,2048]{2,1,0:T(8,128)(2,1)S(1)}, bf16[1,32,2048]{2,1,0:T(8,128)(2,1)S(1)}, u32[]{:S(2)}, u32[]{:S(2)}) collective-permute-start(bf16[1,32,2048]{2,1,0:T(8,128)(2,1)S(1)} %get-tuple-element.15), channel_id=1, source_target_pairs={{0,22},{2,20},{4,18},{6,16},{8,30},{10,28},{12,26},{14,24},{16,6},... | collective-permute-start | bytes 393224 | tf_op jit(solution)/shard_map/ppermute | solution.py:30
  273.8 26.3 %collective-permute-start.11 = (bf16[1,32,2048]{2,1,0:T(8,128)(2,1)S(1)}, bf16[1,32,2048]{2,1,0:T(8,128)(2,1)S(1)}, u32[]{:S(2)}, u32[]{:S(2)}) collective-permute-start(bf16[1,32,2048]{2,1,0:T(8,128)(2,1)S(1)} %get-tuple-element.14), channel_id=1, source_target_pairs={{0,24},{2,26},{4,28},{6,30},{8,16},{10,18},{12,20},{14,22},{16,8},... | collective-permute-start | bytes 393224 | tf_op jit(solution)/shard_map/ppermute | solution.py:30
  275.6 27.7 %collective-permute-start.12 = (bf16[1,32,2048]{2,1,0:T(8,128)(2,1)S(1)}, bf16[1,32,2048]{2,1,0:T(8,128)(2,1)S(1)}, u32[]{:S(2)}, u32[]{:S(2)}) collective-permute-start(bf16[1,32,2048]{2,1,0:T(8,128)(2,1)S(1)} %get-tuple-element.13), channel_id=1, source_target_pairs={{0,26},{2,24},{4,30},{6,28},{8,18},{10,16},{12,22},{14,20},{16,10}... | collective-permute-start | bytes 393224 | tf_op jit(solution)/shard_map/ppermute | solution.py:30
  285.9 19.8 %collective-permute-start.13 = (bf16[1,32,2048]{2,1,0:T(8,128)(2,1)S(1)}, bf16[1,32,2048]{2,1,0:T(8,128)(2,1)S(1)}, u32[]{:S(2)}, u32[]{:S(2)}) collective-permute-start(bf16[1,32,2048]{2,1,0:T(8,128)(2,1)S(1)} %get-tuple-element.12), channel_id=1, source_target_pairs={{0,28},{2,30},{4,24},{6,26},{8,20},{10,22},{12,16},{14,18},{16,12}... | collective-permute-start | bytes 393224 | tf_op jit(solution)/shard_map/ppermute | solution.py:30
  288.7 20.2 %collective-permute-start.14 = (bf16[1,32,2048]{2,1,0:T(8,128)(2,1)S(1)}, bf16[1,32,2048]{2,1,0:T(8,128)(2,1)S(1)}, u32[]{:S(2)}, u32[]{:S(2)}) collective-permute-start(bf16[1,32,2048]{2,1,0:T(8,128)(2,1)S(1)} %get-tuple-element.11), channel_id=1, source_target_pairs={{0,30},{2,28},{4,26},{6,24},{8,22},{10,20},{12,18},{14,16},{16,14}... | collective-permute-start | bytes 393224 | tf_op jit(solution)/shard_map/ppermute | solution.py:30
  313.2 4.3 %copy-start.4 = (f32[32,8]{1,0:T(8,128)S(1)}, f32[32,8]{1,0:T(8,128)}, u32[]{:S(2)}) copy-start(f32[32,8]{1,0:T(8,128)} %copy.90) | copy-start | bytes 3076
  313.2 5.4 %copy-start.7 = (f32[2048]{0:T(1024)S(1)}, f32[2048]{0:T(1024)}, u32[]{:S(2)}) copy-start(f32[2048]{0:T(1024)} %param.29) | copy-start | bytes 24580
Sparse Core Ops, SparseCore 0:
  48.2 29.6 all-reduce.1
  195.4 53.2 reduce-scatter.1
